TPU v7x, 32 devices: a whole 2x2x4 slice. The times are simulated.
32 devices in a mesh: row: 4 (over x, core), col: 8 (over z, y).
Axes of the slice: x: 2, y: 2, z: 4, core: 2. Of those that a mesh axis runs over, the one named last changes fastest.
Arguments:
- centres: float32 [65536, 64], P(('row', 'col')), may hold values from -6 to 6
- weights: float32 [65536, 64], P(('row', 'col')), may hold values from -0.25 to 0.25
- targets: float32 [512, 64], replicated, may hold values from -6 to 6
- batch_index: int32 [512], replicated, may hold values from 0 to 65535
- nystrom_index: int32 [4096], replicated, may hold values from 0 to 65535
- eigvecs: float32 [4096, 1024], P('row', 'col'), may hold values from -0.09375 to 0.09375
- mode_scale: float32 [1024], P('col'), may hold values from 0.02 to 0.2
Outputs:
- residual: float32 [512, 64], replicated
- step: float32 [65536, 64], P(('row', 'col'))
All inputs are finite; a program needn't handle non-finite values.
Results may differ from a plain program's by a relative error of at most 0.0001.
Values sent between devices are 32-bit elements; how exact they have to be, the bound alone decides.
A program may use at most 128 MiB of HBM per device.

v0:
```python
import jax
import jax.numpy as jnp
from jax import lax
from jax.sharding import PartitionSpec as P

learning_rate = 0.25


def kernel(left, right):
    left_sq = jnp.sum(left * left, axis=1)
    right_sq = jnp.sum(right * right, axis=1)
    inner_prod = jnp.dot(
        left, right.T, precision=lax.Precision.HIGHEST, preferred_element_type=jnp.float32
    )
    return jnp.exp(
        -(left_sq[:, None] + right_sq[None, :] - 2.0 * inner_prod) / float(left.shape[1])
    )


def product(left, right):
    return jnp.dot(left, right, precision=lax.Precision.HIGHEST, preferred_element_type=jnp.float32)


def local(centres, weights, targets, batch_index, nystrom_index, eigvecs, mode_scale):
    rows_dev = centres.shape[0]
    block_rows = eigvecs.shape[0]
    offset = lax.axis_index(("row", "col")) * rows_dev

    def select_rows(index):
        local_rows = index - offset
        inside = (local_rows >= 0) & (local_rows < rows_dev)
        fetched = jnp.take(centres, jnp.clip(local_rows, 0, rows_dev - 1), axis=0)
        return jnp.where(inside[:, None], fetched, 0.0)

    batch_feats, nystrom = lax.psum(
        (select_rows(batch_index), select_rows(nystrom_index)), ("row", "col")
    )
    nys_block = lax.dynamic_slice_in_dim(nystrom, lax.axis_index("row") * block_rows, block_rows, 0)
    kern_batch = kernel(centres, batch_feats)
    partial_pred = lax.dot_general(
        kern_batch,
        weights,
        (((0,), (0,)), ((), ())),
        precision=lax.Precision.HIGHEST,
        preferred_element_type=jnp.float32,
    )
    prediction = lax.psum(partial_pred, ("row", "col"))
    residual = prediction - targets
    gradient = product(kernel(nys_block, batch_feats), residual)
    mode_terms = lax.dot_general(
        eigvecs,
        gradient,
        (((0,), (0,)), ((), ())),
        precision=lax.Precision.HIGHEST,
        preferred_element_type=jnp.float32,
    )
    coeff = mode_scale[:, None] * lax.psum(mode_terms, "row")
    correction = lax.psum(product(eigvecs, coeff), "col")
    direct = product(kern_batch, residual)
    folded = direct - product(
        kernel(centres, nystrom), lax.all_gather(correction, "row", axis=0, tiled=True)
    )
    step = learning_rate * folded
    return (residual, step)


def solution(mesh):
    in_specs = (
        P(("row", "col"), None),
        P(("row", "col"), None),
        P(),
        P(),
        P(),
        P("row", "col"),
        P("col"),
    )
    out_specs = (P(), P(("row", "col"), None))
    return jax.shard_map(local, mesh=mesh, in_specs=in_specs, out_specs=out_specs, check_vma=False)
```

profile of v0, /device:TPU:0, one launch (start us, length us, event | category | flops | bytes accessed | tf_op | source)
XLA Modules:
  0.0 467.1 jit_solution(167002956576013100)
XLA Ops:
  7.2 0.0 copy-start
  7.2 0.0 all-reduce.5.cloned.1.call-start
  7.2 0.7 compare_and_fusion.2
  8.0 0.0 copy-start.8
  8.0 1.4 copy.9
  9.4 1.0 gather_fusion
  10.4 0.9 select_select_fusion.1
  11.3 0.0 all-reduce.5.cloned.1.call-update
  11.4 0.0 all-reduce.9.cloned.1.call-start
  11.4 0.0 copy-done.8
  11.5 14.2 %gather_fusion.1 = f32[4096,64]{1,0:T(8,128)} fusion(f32[2048,64]{1,0:T(8,128)S(1)} %copy.9, s32[4096]{0:T(1024)S(1)} %fusion.30), kind=kCustom, calls=%fused_computation.1 | custom fusion | bytes 2113536 | tf_op jit(solution)/shard_map/jit(_take)/gather | solution.py:32
  25.7 0.0 copy-start.3
  25.7 6.0 %select_select_fusion = f32[4096,64]{1,0:T(8,128)} fusion(f32[4096,64]{1,0:T(8,128)} %gather_fusion.1, pred[4096]{0:T(1024)(128)(4,1)S(1)} %get-tuple-element.7, pred[4096]{0:T(1024)(128)(4,1)S(1)} %get-tuple-element.6), kind=kLoop, calls=%fused_computation.27 | loop fusion | flops 524288 | bytes 2105344 | tf_op jit(solution)/shard_map/jit(_where)/select_n | solution.py:33
  31.7 0.0 copy-done.3
  31.7 0.1 multiply_reduce_fusion.2
  31.8 111.6 %all-reduce.5.cloned.1.call-done = f32[512,64]{1,0:T(8,128)} async-done(((f32[512,64]{1,0:T(8,128)}), f32[512,64]{1,0:T(8,128)}) %all-reduce.5.cloned.1.call-update) | async-done | bytes 131088 | tf_op jit(solution)/shard_map/psum | solution.py:35
  143.3 1.1 multiply_reduce_fusion.3
  144.4 0.0 copy-start.5
  144.4 5.1 %fusion.13 = f32[2048,512]{0,1:T(8,128)S(1)} fusion(f32[512,64]{1,0:T(8,128)} %all-reduce.5.cloned.1.call-done, f32[2048,64]{0,1:T(8,128)S(1)} %copy-done.3, f32[512]{0:T(512)S(1)} %multiply_reduce_fusion.3, f32[2048]{0:T(1024)S(1)} %multiply_reduce_fusion.2), kind=kOutput, calls=%fused_computation.16 | convolution fusion | flops 810549248 | bytes 4859904 | tf_op jit(solution)/shard_map/dot_general | solution.py:12
  149.5 0.0 copy-start.1
  149.5 2.0 copy-done.1
  151.6 0.0 copy-done.5
  151.6 4.8 %fusion.36 = f32[512,64]{0,1:T(8,128)} fusion(f32[2048,512]{0,1:T(8,128)S(1)} %fusion.13, f32[2048,64]{0,1:T(8,128)S(1)} %copy-done.5), kind=kOutput, calls=%fused_computation.55 | convolution fusion | flops 805306368 | bytes 4849664 | tf_op jit(solution)/shard_map/dot_general | solution.py:40
  156.4 0.0 copy-start.7
  156.4 0.0 copy-start.4
  156.4 0.0 all-reduce.9.cloned.1.call-update
  156.4 0.2 all-reduce.7.cloned.1.call-start
  156.7 134.4 %all-reduce.9.cloned.1.call-done = (f32[512,64]{0,1:T(8,128)}, f32[4096,64]{1,0:T(8,128)}) async-done(((f32[512,64]{0,1:T(8,128)}, f32[4096,64]{1,0:T(8,128)}), (f32[512,64]{0,1:T(8,128)}, f32[4096,64]{1,0:T(8,128)})) %all-reduce.9.cloned.1.call-update) | async-done | bytes 1179664 | tf_op jit(solution)/shard_map/psum | solution.py:47
  291.1 0.0 copy-done.7
  291.1 0.9 sub.30
  292.0 0.0 copy-start.6
  292.0 1.3 multiply_reduce_fusion.1
  293.3 0.0 copy-done.4
  293.3 2.8 fusion.26
  296.2 0.0 copy-start.9
  296.2 0.0 copy-start.2
  296.2 2.1 fusion.15
  298.3 0.0 copy-done
  298.3 1.0 convolution_bitcast_fusion.1
  299.3 10.7 %psum.38 = f32[128,64]{1,0:T(8,128)S(1)} all-reduce(f32[128,64]{1,0:T(8,128)S(1)} %convolution_bitcast_fusion.1), channel_id=1, replica_groups=mesh['row'=4,'col'=8] {'row'}, use_global_device_ids=true, to_apply=%region_7.8 | all-reduce | flops 8192 | bytes 65536 | tf_op jit(solution)/shard_map/psum | solution.py:57
  310.0 0.0 copy-done.9
  310.0 1.5 convolution_bitcast_fusion
  311.4 0.0 all-reduce.7.cloned.1.call-update
  311.5 0.3 all-gather.2.cloned.1.call-start
  311.7 0.0 copy-done.2
  311.8 0.6 multiply_reduce_fusion
  312.4 69.5 %all-reduce.7.cloned.1.call-done = f32[1024,64]{0,1:T(8,128)} async-done(((f32[1024,64]{0,1:T(8,128)}), f32[1024,64]{0,1:T(8,128)}) %all-reduce.7.cloned.1.call-update) | async-done | bytes 262160 | tf_op jit(solution)/shard_map/psum | solution.py:58
  381.9 0.0 all-gather.2.cloned.1.call-update
  381.9 30.2 %fusion.37 = f32[4096,2048]{0,1:T(8,128)} fusion(f32[4096,64]{1,0:T(8,128)S(1)} %copy-done.2, f32[2048,64]{0,1:T(8,128)S(1)} %copy-done.3), kind=kOutput, calls=%fused_computation.56 | convolution fusion | flops 6442450944 | bytes 35127296 | tf_op jit(solution)/shard_map/dot_general | solution.py:12
  412.1 0.0 all-gather.2.cloned.1.call-done
  412.1 42.7 %fusion.3 = f32[2048,64]{0,1:T(8,128)S(1)} fusion(f32[4096,64]{0,1:T(8,128)} %all-gather.2.cloned.1.call-done, f32[4096,2048]{0,1:T(8,128)} %fusion.37, f32[4096]{0:T(1024)S(1)} %multiply_reduce_fusion, f32[2048]{0:T(1024)S(1)} %multiply_reduce_fusion.2), kind=kOutput, calls=%fused_computation.6 | convolution fusion | flops 6484393984 | bytes 35151872 | tf_op jit(solution)/shard_map/dot_general | solution.py:21
  454.8 0.0 copy-done.6
  454.8 5.8 %fusion.14 = f32[2048,64]{0,1:T(8,128)} fusion(f32[2048,64]{0,1:T(8,128)S(1)} %fusion.3, f32[2048,512]{0,1:T(8,128)} %copy-done.1, f32[512,64]{0,1:T(8,128)S(1)} %sub.30), kind=kOutput, calls=%fused_computation.18 | convolution fusion | flops 805568512 | bytes 5373952 | tf_op jit(solution)/shard_map/dot_general | solution.py:21
  (3 shorter events, 0.0 us)
Async XLA Ops:
  7.2 291.1 %copy-start = (f32[1024,128]{1,0:T(8,128)S(1)}, f32[1024,128]{1,0:T(8,128)}, u32[]{:S(2)}) copy-start(f32[1024,128]{1,0:T(8,128)} %param.12) | copy-start | bytes 1572868
  7.2 136.2 %all-reduce.5.cloned.1.call-start = ((), (), s32[]{:S(2)}) async-start(), calls=%async_computation | async-start | bytes 524288 | tf_op jit(solution)/shard_map/psum | solution.py:35
  8.0 3.4 copy-start.8
  11.4 279.7 %all-reduce.9.cloned.1.call-start = ((), (), s32[]{:S(2)}) async-start(), calls=%async_computation.3 | async-start | bytes 4456448 | tf_op jit(solution)/shard_map/psum | solution.py:47
  25.7 6.0 %copy-start.3 = (f32[2048,64]{0,1:T(8,128)S(1)}, f32[2048,64]{0,1:T(8,128)}, u32[]{:S(2)}) copy-start(f32[2048,64]{0,1:T(8,128)} %param.7) | copy-start | bytes 1572868
  144.4 7.1 %copy-start.5 = (f32[2048,64]{0,1:T(8,128)S(1)}, f32[2048,64]{0,1:T(8,128)}, u32[]{:S(2)}) copy-start(f32[2048,64]{0,1:T(8,128)} %param.8) | copy-start | bytes 1572868
  149.5 2.0 copy-start.1
  156.4 134.7 %copy-start.7 = (f32[512,64]{0,1:T(8,128)S(1)}, f32[512,64]{0,1:T(8,128)}, u32[]{:S(2)}) copy-start(f32[512,64]{0,1:T(8,128)} %param.9) | copy-start | bytes 393220
  156.4 136.9 %copy-start.4 = (f32[512,64]{1,0:T(8,128)S(1)}, f32[512,64]{1,0:T(8,128)}, u32[]{:S(2)}) copy-start(f32[512,64]{1,0:T(8,128)} %all-reduce.5.cloned.1.call-done) | copy-start | bytes 393220
  156.4 225.5 %all-reduce.7.cloned.1.call-start = ((), (), s32[]{:S(2)}) async-start(), calls=%async_computation.1 | async-start | bytes 524288 | tf_op jit(solution)/shard_map/psum | solution.py:58
  292.0 162.8 %copy-start.6 = (f32[512,64]{0,1:T(8,128)}, f32[512,64]{0,1:T(8,128)S(1)}, u32[]{:S(2)}) copy-start(f32[512,64]{0,1:T(8,128)S(1)} %sub.30) | copy-start | bytes 393220
  296.2 13.8 %copy-start.9 = (f32[128]{0:T(128)S(1)}, f32[128]{0:T(128)}, u32[]{:S(2)}) copy-start(f32[128]{0:T(128)} %param.13) | copy-start | bytes 1540
  296.2 15.5 %copy-start.2 = (f32[4096,64]{1,0:T(8,128)S(1)}, f32[4096,64]{1,0:T(8,128)}, u32[]{:S(2)}) copy-start(f32[4096,64]{1,0:T(8,128)} %get-tuple-element.3) | copy-start | bytes 3145732
  311.5 100.6 %all-gather.2.cloned.1.call-start = ((), (), s32[]{:S(2)}) async-start(), calls=%async_computation.2 | async-start | bytes 1310720 | tf_op jit(solution)/shard_map/all_gather | solution.py:61
Sparse Core Ops, SparseCore 0:
  14.1 129.2 all-reduce.4
  156.6 134.4 all-reduce.8
  311.6 70.2 all-reduce.6
  383.3 15.8 all-gather.1
where the time goes:
time: 468 us; the launch traced here: 467 us
  waiting for transfers between devices  316 us (68%)
  matrix products  95.9 us (20%)
  local copies, waits for them, and re-layouts  18.7 us (4%)
  between operations  14 us (3%)
  other arithmetic  11.7 us (2%)
  blocking collectives  10.7 us (2%)
    psum x1, waiting for transfers between devices, local(): prediction = lax.psum(partial_pred, ('row', 'col'))  134 us
    psum x1, waiting for transfers between devices, local(): lax.psum((select_rows(batch_index), select_rows(nystrom_index)), ('row',...  112 us
    psum x1, waiting for transfers between devices, local(): correction = lax.psum(product(eigvecs, coeff), 'col')  69.5 us
    dot_general x4, matrix products, product(): jnp.dot(left, right, precision=lax.Precision.HIGHEST, preferred_element_t...  52 us
    dot_general x3, matrix products, kernel(): jnp.dot(left, right.T, precision=lax.Precision.HIGHEST, preferred_element...  38.1 us
    gather x2, local copies, waits for them, and re-layouts, select_rows(): fetched = jnp.take(centres, jnp.clip(local_rows, 0, rows_dev - 1), axis=0)  15.2 us
    psum x1, blocking collectives, local(): coeff = mode_scale[:, None] * lax.psum(mode_terms, 'row')  10.7 us
  transfers between devices with their start and end apart: 4, of which 3 were waited for; matrix products, arithmetic and copies ran while one was open for 11% of the time, Pallas kernels for 0%

commit v1 on v0

--- a/solution.py
+++ b/solution.py
@@ -33,7 +33,7 @@
         return jnp.where(inside[:, None], fetched, 0.0)
 
     batch_feats, nystrom = lax.psum(
-        (select_rows(batch_index), select_rows(nystrom_index)), ("row", "col")
+        lax.psum((select_rows(batch_index), select_rows(nystrom_index)), "col"), "row"
     )
     nys_block = lax.dynamic_slice_in_dim(nystrom, lax.axis_index("row") * block_rows, block_rows, 0)
     kern_batch = kernel(centres, batch_feats)

time: 468 us -> 513 us (1.096)
  waiting for transfers between devices: 316 us -> 359 us
    psum x1 -> x2, waiting for transfers between devices: 112 us -> 169 us  [the longest x1 111 us: local(): lax.psum((select_rows(batch_index), select_rows(nystrom_index)), 'col')]
    psum x1, waiting for transfers between devices: 134 us -> 121 us  [local(): prediction = lax.psum(partial_pred, ('row', 'col'))]
  transfers between devices with their start and end apart: 4 -> 5, of which waited for: 3 -> 4; matrix products, arithmetic and copies ran while one was open for 11% -> 7% of each run, Pallas kernels for 0% -> 0%
where the time goes in v1:
time: 513 us
  waiting for transfers between devices  359 us (70%)
  matrix products  97.8 us (19%)
  local copies, waits for them, and re-layouts  18.6 us (4%)
  between operations  14 us (3%)
  other arithmetic  11.9 us (2%)
  blocking collectives  10.7 us (2%)
    psum x1, waiting for transfers between devices, local(): prediction = lax.psum(partial_pred, ('row', 'col'))  121 us
    psum x1, waiting for transfers between devices, local(): lax.psum((select_rows(batch_index), select_rows(nystrom_index)), 'col')  111 us
    psum x1, waiting for transfers between devices, local(): correction = lax.psum(product(eigvecs, coeff), 'col')  69.6 us
    psum x1, waiting for transfers between devices, local(): lax.psum(lax.psum((select_rows(batch_index), select_rows(nystrom_index)),...  57.1 us
    dot_general x4, matrix products, product(): jnp.dot(left, right, precision=lax.Precision.HIGHEST, preferred_element_t...  53.7 us
    dot_general x3, matrix products, kernel(): jnp.dot(left, right.T, precision=lax.Precision.HIGHEST, preferred_element...  38.3 us
    gather x2, local copies, waits for them, and re-layouts, select_rows(): fetched = jnp.take(centres, jnp.clip(local_rows, 0, rows_dev - 1), axis=0)  15.1 us
    psum x1, blocking collectives, local(): coeff = mode_scale[:, None] * lax.psum(mode_terms, 'row')  10.7 us
  transfers between devices with their start and end apart: 5, of which 4 were waited for; matrix products, arithmetic and copies ran while one was open for 7% of the time, Pallas kernels for 0%

profile of v1, /device:TPU:0, one launch (start us, length us, event | category | flops | bytes accessed | tf_op | source)
XLA Modules:
  0.0 512.9 jit_solution(337708901357331131)
XLA Ops:
  7.2 0.0 copy-start
  7.2 0.0 all-reduce.11.cloned.1.call-start
  7.2 0.8 compare_and_fusion.1
  8.0 0.7 fusion.30
  8.8 0.7 compare_and_fusion.2
  9.5 1.4 copy.9
  10.8 1.0 gather_fusion
  11.9 14.1 %gather_fusion.1 = f32[4096,64]{1,0:T(8,128)} fusion(f32[2048,64]{1,0:T(8,128)S(1)} %copy.9, s32[4096]{0:T(1024)S(1)} %fusion.30), kind=kCustom, calls=%fused_computation.1 | custom fusion | bytes 2113536 | tf_op jit(solution)/shard_map/jit(_take)/gather | solution.py:32
  26.0 0.9 select_select_fusion.1
  26.9 5.9 %select_select_fusion = f32[4096,64]{1,0:T(8,128)} fusion(f32[4096,64]{1,0:T(8,128)} %gather_fusion.1, pred[4096]{0:T(1024)(128)(4,1)S(1)} %get-tuple-element.9, pred[4096]{0:T(1024)(128)(4,1)S(1)} %get-tuple-element.8), kind=kLoop, calls=%fused_computation.27 | loop fusion | flops 524288 | bytes 2105344 | tf_op jit(solution)/shard_map/jit(_where)/select_n | solution.py:33
  32.8 0.0 copy-start.3
  32.8 0.0 all-reduce.11.cloned.1.call-update
  32.8 0.0 all-reduce.13.cloned.1.call-start
  32.9 111.5 %all-reduce.11.cloned.1.call-done = (f32[512,64]{1,0:T(8,128)}, f32[4096,64]{1,0:T(8,128)}) async-done(((f32[512,64]{1,0:T(8,128)}, f32[4096,64]{1,0:T(8,128)}), (f32[512,64]{1,0:T(8,128)}, f32[4096,64]{1,0:T(8,128)})) %all-reduce.11.cloned.1.call-update) | async-done | bytes 1179664 | tf_op jit(solution)/shard_map/psum | solution.py:36
  144.3 0.0 all-reduce.13.cloned.1.call-update
  144.4 0.0 all-reduce.7.cloned.1.call-start
  144.4 0.0 copy-done.3
  144.4 0.1 multiply_reduce_fusion.2
  144.5 57.1 %all-reduce.13.cloned.1.call-done = (f32[512,64]{1,0:T(8,128)}, f32[4096,64]{1,0:T(8,128)}) async-done(((f32[512,64]{1,0:T(8,128)}, f32[4096,64]{1,0:T(8,128)}), (f32[512,64]{1,0:T(8,128)}, f32[4096,64]{1,0:T(8,128)})) %all-reduce.13.cloned.1.call-update) | async-done | bytes 1179664 | tf_op jit(solution)/shard_map/psum | solution.py:35
  201.6 1.1 multiply_reduce_fusion.3
  202.7 0.0 copy-start.5
  202.7 5.1 fusion.13
  207.8 0.0 copy-start.1
  207.8 2.0 copy-done.1
  209.8 0.0 copy-done.5
  209.8 0.0 copy-start.2
  209.8 0.0 copy-start.4
  209.8 4.8 fusion.36
  214.7 0.0 copy-start.7
  214.7 0.0 all-reduce.7.cloned.1.call-update
  214.7 0.2 all-reduce.9.cloned.1.call-start
  214.9 0.0 copy-done.2
  215.0 0.0 copy-done.4
  215.0 3.1 fusion.26
  218.1 0.2 multiply_reduce_fusion.1
  218.3 121.1 %all-reduce.7.cloned.1.call-done = f32[512,64]{0,1:T(8,128)} async-done(((f32[512,64]{0,1:T(8,128)}), f32[512,64]{0,1:T(8,128)}) %all-reduce.7.cloned.1.call-update) | async-done | bytes 131088 | tf_op jit(solution)/shard_map/psum | solution.py:47
  339.4 0.0 copy-done.7
  339.4 0.9 sub.30
  340.4 0.0 copy-start.6
  340.4 0.0 copy-start.8
  340.4 3.7 fusion.15
  344.1 0.0 copy-done
  344.1 1.0 convolution_bitcast_fusion.1
  345.1 10.7 %psum.54 = f32[128,64]{1,0:T(8,128)S(1)} all-reduce(f32[128,64]{1,0:T(8,128)S(1)} %convolution_bitcast_fusion.1), channel_id=1, replica_groups=mesh['row'=4,'col'=8] {'row'}, use_global_device_ids=true, to_apply=%region_9.10 | all-reduce | flops 8192 | bytes 65536 | tf_op jit(solution)/shard_map/psum | solution.py:57
  355.8 0.0 copy-done.8
  355.9 1.5 convolution_bitcast_fusion
  357.3 0.0 all-reduce.9.cloned.1.call-update
  357.4 0.3 all-gather.2.cloned.1.call-start
  357.6 0.6 multiply_reduce_fusion
  358.2 69.6 %all-reduce.9.cloned.1.call-done = f32[1024,64]{0,1:T(8,128)} async-done(((f32[1024,64]{0,1:T(8,128)}), f32[1024,64]{0,1:T(8,128)}) %all-reduce.9.cloned.1.call-update) | async-done | bytes 262160 | tf_op jit(solution)/shard_map/psum | solution.py:58
  427.8 0.0 all-gather.2.cloned.1.call-update
  427.8 30.1 %fusion.37 = f32[4096,2048]{0,1:T(8,128)} fusion(f32[4096,64]{1,0:T(8,128)S(1)} %copy-done.2, f32[2048,64]{0,1:T(8,128)S(1)} %copy-done.3), kind=kOutput, calls=%fused_computation.56 | convolution fusion | flops 6442450944 | bytes 35127296 | tf_op jit(solution)/shard_map/dot_general | solution.py:12
  457.9 0.0 all-gather.2.cloned.1.call-done
  457.9 42.7 %fusion.3 = f32[2048,64]{0,1:T(8,128)S(1)} fusion(f32[4096,64]{0,1:T(8,128)} %all-gather.2.cloned.1.call-done, f32[4096,2048]{0,1:T(8,128)} %fusion.37, f32[4096]{0:T(1024)S(1)} %multiply_reduce_fusion, f32[2048]{0:T(1024)S(1)} %multiply_reduce_fusion.2), kind=kOutput, calls=%fused_computation.6 | convolution fusion | flops 6484393984 | bytes 35151872 | tf_op jit(solution)/shard_map/dot_general | solution.py:21
  500.6 0.0 copy-done.6
  500.6 5.8 %fusion.14 = f32[2048,64]{0,1:T(8,128)} fusion(f32[2048,64]{0,1:T(8,128)S(1)} %fusion.3, f32[2048,512]{0,1:T(8,128)} %copy-done.1, f32[512,64]{0,1:T(8,128)S(1)} %sub.30), kind=kOutput, calls=%fused_computation.18 | convolution fusion | flops 805568512 | bytes 5373952 | tf_op jit(solution)/shard_map/dot_general | solution.py:21
  (1 shorter events, 0.0 us)
Async XLA Ops:
  7.2 336.9 %copy-start = (f32[1024,128]{1,0:T(8,128)S(1)}, f32[1024,128]{1,0:T(8,128)}, u32[]{:S(2)}) copy-start(f32[1024,128]{1,0:T(8,128)} %param.12) | copy-start | bytes 1572868
  7.2 137.2 %all-reduce.11.cloned.1.call-start = ((), (), s32[]{:S(2)}) async-start(), calls=%async_computation.3 | async-start | bytes 4718592 | tf_op jit(solution)/shard_map/psum | solution.py:36
  32.8 111.6 %copy-start.3 = (f32[2048,64]{0,1:T(8,128)S(1)}, f32[2048,64]{0,1:T(8,128)}, u32[]{:S(2)}) copy-start(f32[2048,64]{0,1:T(8,128)} %param.7) | copy-start | bytes 1572868
  32.8 168.8 %all-reduce.13.cloned.1.call-start = ((), (), s32[]{:S(2)}) async-start(), calls=%async_computation.4 | async-start | bytes 4718592 | tf_op jit(solution)/shard_map/psum | solution.py:35
  144.4 195.1 %all-reduce.7.cloned.1.call-start = ((), (), s32[]{:S(2)}) async-start(), calls=%async_computation | async-start | bytes 262144 | tf_op jit(solution)/shard_map/psum | solution.py:47
  202.7 7.1 %copy-start.5 = (f32[2048,64]{0,1:T(8,128)S(1)}, f32[2048,64]{0,1:T(8,128)}, u32[]{:S(2)}) copy-start(f32[2048,64]{0,1:T(8,128)} %param.8) | copy-start | bytes 1572868
  207.8 2.0 copy-start.1
  209.8 5.1 copy-start.2
  209.8 5.1 copy-start.4
  214.7 124.7 %copy-start.7 = (f32[512,64]{0,1:T(8,128)S(1)}, f32[512,64]{0,1:T(8,128)}, u32[]{:S(2)}) copy-start(f32[512,64]{0,1:T(8,128)} %param.9) | copy-start | bytes 393220
  214.7 213.1 %all-reduce.9.cloned.1.call-start = ((), (), s32[]{:S(2)}) async-start(), calls=%async_computation.1 | async-start | bytes 524288 | tf_op jit(solution)/shard_map/psum | solution.py:58
  340.4 160.3 %copy-start.6 = (f32[512,64]{0,1:T(8,128)}, f32[512,64]{0,1:T(8,128)S(1)}, u32[]{:S(2)}) copy-start(f32[512,64]{0,1:T(8,128)S(1)} %sub.30) | copy-start | bytes 393220
  340.4 15.5 %copy-start.8 = (f32[128]{0:T(128)S(1)}, f32[128]{0:T(128)}, u32[]{:S(2)}) copy-start(f32[128]{0:T(128)} %param.13) | copy-start | bytes 1540
  357.4 100.5 %all-gather.2.cloned.1.call-start = ((), (), s32[]{:S(2)}) async-start(), calls=%async_computation.2 | async-start | bytes 1310720 | tf_op jit(solution)/shard_map/all_gather | solution.py:61
Sparse Core Ops, SparseCore 0:
  33.0 111.3 all-reduce.10
  146.8 54.8 all-reduce.12
  214.8 124.5 all-reduce.6
  357.5 70.2 all-reduce.8
  429.2 15.8 all-gather.1
